TPU v7x, 32 devices: a whole 2x2x4 slice. The times are simulated.
32 devices in a mesh: kpt: 2 (over y), pert: 4 (over z), pw: 4 (over x, core).
Axes of the slice: x: 2, y: 2, z: 4, core: 2. Of those that a mesh axis runs over, the one named last changes fastest.
Arguments:
- occupied: bfloat16 [3072, 8192], P(('kpt', 'pert'), 'pw'), parts along dimension 0, may hold values from -0.0625 to 0.0625
- response: bfloat16 [8, 128, 8192], P(('kpt', 'pert'), None, 'pw'), parts along dimension 0, may hold values from -6 to 6
Outputs:
- correlation: float32 [8, 128, 1536], P(('kpt', 'pert')), parts along dimension 0
- projected: float32 [8, 128, 8192], P(('kpt', 'pert'), None, 'pw'), parts along dimension 0
There are 2 independent parts, one for each index of `kpt`. A program takes and returns all parts, laid end to end along the dimension named above; each array names one. Nothing has to cross between parts.
All inputs are finite; a program needn't handle non-finite values.
Results may differ from a plain program's by a relative error of at most 0.00096.
Values may be sent and summed in bfloat16 or wider, within the bound.
No kernel may reach another device: no remote copies, remote signals or barrier semaphores. Data moves between devices by JAX's collectives and lax.ppermute only.
A program may use at most 64 MiB of HBM per device.

v0:
```python
import jax
import jax.numpy as jnp
from jax import lax
from jax.sharding import PartitionSpec as P


def from_behind(block, axis, distance):
    devices = range(lax.axis_size(axis))
    route = [((i - distance) % len(devices), i) for i in devices]
    return lax.ppermute(block, axis, route)


def local(occupied, response):
    rows = response.reshape(-1, response.shape[-1])
    band_local = occupied.shape[0]
    cycle_size = lax.axis_size("pert")
    total_bands = band_local * cycle_size
    zero_index = jnp.zeros((), jnp.int32)
    empty_correlation = jnp.zeros((rows.shape[0], total_bands), jnp.float32)
    empty_correction = jnp.zeros(rows.shape, jnp.float32)
    position = lax.axis_index("pert")

    def visit(step, piece, correlation, correction):
        owner = (position - step) % cycle_size
        start = owner * band_local
        part = lax.dot_general(
            rows, piece, (((1,), (1,)), ((), ())), preferred_element_type=jnp.float32
        )
        summed = lax.psum(part, "pw")
        correlation = lax.dynamic_update_slice(correlation, summed, (zero_index, start))
        correction = correction + jnp.dot(
            summed.astype(jnp.bfloat16), piece, preferred_element_type=jnp.float32
        )
        return (correlation, correction)

    def turn(step, state):
        piece, correlation, correction = state
        correlation, correction = visit(step, piece, correlation, correction)
        piece = from_behind(piece, "pert", 1)
        return (piece, correlation, correction)

    piece, correlation, correction = lax.fori_loop(
        0, cycle_size - 1, turn, (occupied, empty_correlation, empty_correction)
    )
    correlation, correction = visit(cycle_size - 1, piece, correlation, correction)
    projected = rows.astype(jnp.float32) - correction
    correlation_out = correlation.reshape(response.shape[0], response.shape[1], total_bands)
    return (correlation_out, projected.reshape(response.shape))


def solution(mesh):
    in_specs = (P(("kpt", "pert"), "pw"), P(("kpt", "pert"), None, "pw"))
    out_specs = (P(("kpt", "pert"), None, None), P(("kpt", "pert"), None, "pw"))
    return jax.shard_map(local, mesh=mesh, in_specs=in_specs, out_specs=out_specs, check_vma=False)
```

profile of v0, /device:TPU:0, one launch (start us, length us, event | category | flops | bytes accessed | tf_op | source)
XLA Modules:
  0.0 176.5 jit_solution(3041188094833959325)
XLA Ops:
  8.0 1.0 broadcast_in_dim.6
  9.0 0.7 copy-done
  9.7 120.9 %while.20 = (s32[]{:T(128)}, bf16[384,2048]{1,0:T(8,128)(2,1)S(1)}, f32[128,1536]{1,0:T(8,128)}, f32[128,2048]{1,0:T(8,128)}, bf16[128,2048]{1,0:T(8,128)(2,1)},...) while((s32[]{:T(128)}, bf16[384,2048]{1,0:T(8,128)(2,1)S(1)}, ...), condition=%wide.region_2.3_spmd.clone, body=%wide.region_0.2_spmd.clone.sunk | while | flops 403275776 | bytes 19267988 | solution.py:42
  9.7 0.2 copy.12
  9.9 3.1 %collective-permute-start = (bf16[384,2048]{1,0:T(8,128)(2,1)S(1)}, bf16[384,2048]{1,0:T(8,128)(2,1)S(1)}, u32[]{:S(2)}, u32[]{:S(2)}) collective-permute-start(bf16[384,2048]{1,0:T(8,128)(2,1)S(1)} %copy.12), channel_id=1, source_target_pairs={{12,0},{0,4},{4,8},{8,12},{13,1},{1,5},{5,9},{9,13},{14,2},{2,6},{... | collective-permute-start | bytes 4718600 | tf_op jit(solution)/shard_map/while/body/eval_jaxpr/ppermute | solution.py:10
  13.0 1.3 fusion.20
  14.3 0.0 all-reduce.5.cloned.1.call-update
  14.3 33.2 %all-reduce.5.cloned.1.call-done = f32[128,384]{1,0:T(8,128)} async-done(((f32[128,384]{1,0:T(8,128)}), f32[128,384]{1,0:T(8,128)}) %all-reduce.5.cloned.1.call-update) | async-done | bytes 196624 | tf_op jit(solution)/shard_map/while/body/eval_jaxpr/psum | solution.py:29
  47.6 1.6 constant_dynamic-update-slice_fusion.3
  49.2 2.3 %convolution_add_fusion.3 = f32[128,2048]{1,0:T(8,128)} fusion(bf16[384,2048]{1,0:T(8,128)(2,1)S(1)} %copy.12, f32[128,2048]{1,0:T(8,128)} %get-tuple-element.247, pred[]{:T(512)S(6)} %compare.5, f32[128,384]{1,0:T(8,128)} %all-reduce.5.cloned.1.call-done), kind=kOutput, calls=%fused_computation.clone.1 | convolution fusion | flops 201900032 | bytes 3866625 | tf_op jit(solution)/shard_map/while/body/eval_jaxpr/dot_general | solution.py:31
  51.5 0.2 copy.12
  51.7 1.5 collective-permute-start
  53.2 1.3 fusion.20
  54.5 0.0 all-reduce.5.cloned.1.call-update
  54.6 32.1 %all-reduce.5.cloned.1.call-done = f32[128,384]{1,0:T(8,128)} async-done(((f32[128,384]{1,0:T(8,128)}), f32[128,384]{1,0:T(8,128)}) %all-reduce.5.cloned.1.call-update) | async-done | bytes 196624 | tf_op jit(solution)/shard_map/while/body/eval_jaxpr/psum | solution.py:29
  86.7 1.6 constant_dynamic-update-slice_fusion.3
  88.3 2.8 %convolution_add_fusion.3 = f32[128,2048]{1,0:T(8,128)} fusion(bf16[384,2048]{1,0:T(8,128)(2,1)S(1)} %copy.12, f32[128,2048]{1,0:T(8,128)} %get-tuple-element.247, pred[]{:T(512)S(6)} %compare.5, f32[128,384]{1,0:T(8,128)} %all-reduce.5.cloned.1.call-done), kind=kOutput, calls=%fused_computation.clone.1 | convolution fusion | flops 201900032 | bytes 3866625 | tf_op jit(solution)/shard_map/while/body/eval_jaxpr/dot_general | solution.py:31
  91.1 0.2 copy.12
  91.3 1.5 collective-permute-start
  92.8 1.3 fusion.20
  94.1 0.0 all-reduce.5.cloned.1.call-update
  94.2 32.1 %all-reduce.5.cloned.1.call-done = f32[128,384]{1,0:T(8,128)} async-done(((f32[128,384]{1,0:T(8,128)}), f32[128,384]{1,0:T(8,128)}) %all-reduce.5.cloned.1.call-update) | async-done | bytes 196624 | tf_op jit(solution)/shard_map/while/body/eval_jaxpr/psum | solution.py:29
  126.3 1.6 constant_dynamic-update-slice_fusion.3
  127.9 2.8 %convolution_add_fusion.3 = f32[128,2048]{1,0:T(8,128)} fusion(bf16[384,2048]{1,0:T(8,128)(2,1)S(1)} %copy.12, f32[128,2048]{1,0:T(8,128)} %get-tuple-element.247, pred[]{:T(512)S(6)} %compare.5, f32[128,384]{1,0:T(8,128)} %all-reduce.5.cloned.1.call-done), kind=kOutput, calls=%fused_computation.clone.1 | convolution fusion | flops 201900032 | bytes 3866625 | tf_op jit(solution)/shard_map/while/body/eval_jaxpr/dot_general | solution.py:31
  130.6 0.0 collective-permute-done
  130.6 0.0 copy-start.3
  130.7 2.4 %convolution_bitcast_fusion = f32[128,384]{0,1:T(8,128)} fusion(bf16[384,2048]{1,0:T(8,128)(2,1)S(1)} %get-tuple-element.160, bf16[1,128,2048]{2,1,0:T(8,128)(2,1)} %bitcast.22), kind=kOutput, calls=%fused_computation.6 | convolution fusion | flops 201326592 | bytes 2293760 | tf_op jit(solution)/shard_map/dot_general | solution.py:26
  133.1 0.0 all-reduce.3.cloned.1.call-update
  133.1 32.1 %all-reduce.3.cloned.1.call-done = f32[128,384]{0,1:T(8,128)} async-done(((f32[128,384]{0,1:T(8,128)}), f32[128,384]{0,1:T(8,128)}) %all-reduce.3.cloned.1.call-update) | async-done | bytes 196624 | tf_op jit(solution)/shard_map/psum | solution.py:29
  165.3 1.1 copy.4
  166.3 0.7 constant_dynamic-update-slice_fusion.1
  167.0 2.4 %fusion.2 = f32[1,128,2048]{2,1,0:T(8,128)} fusion(f32[128,2048]{1,0:T(8,128)S(1)} %copy-done.1, bf16[384,2048]{1,0:T(8,128)(2,1)S(1)} %get-tuple-element.160, f32[128,384]{0,1:T(8,128)} %all-reduce.3.cloned.1.call-done, bf16[1,128,2048]{2,1,0:T(8,128)(2,1)S(1)} %bitcast.23), kind=kOutput, calls=%fused_computation.5 | convolution fusion | flops 202162176 | bytes 4390912 | tf_op jit(solution)/shard_map/dot_general | solution.py:31
  (17 shorter events, 0.0 us)
Async XLA Ops:
  8.0 1.7 copy-start
  9.7 37.9 %all-reduce.5.cloned.1.call-start = ((), (), s32[]{:S(2)}) async-start(), calls=%async_computation.1 | async-start | bytes 393216 | tf_op jit(solution)/shard_map/while/body/eval_jaxpr/psum | solution.py:29
  9.7 3.3 %copy-start.2 = (bf16[128,2048]{1,0:T(8,128)(2,1)S(1)}, bf16[128,2048]{1,0:T(8,128)(2,1)}, u32[]{:S(2)}) copy-start(bf16[128,2048]{1,0:T(8,128)(2,1)} %get-tuple-element.260) | copy-start | bytes 1572868 | tf_op jit(solution)/shard_map/while
  9.9 41.7 %collective-permute-start = (bf16[384,2048]{1,0:T(8,128)(2,1)S(1)}, bf16[384,2048]{1,0:T(8,128)(2,1)S(1)}, u32[]{:S(2)}, u32[]{:S(2)}) collective-permute-start(bf16[384,2048]{1,0:T(8,128)(2,1)S(1)} %copy.12), channel_id=1, source_target_pairs={{12,0},{0,4},{4,8},{8,12},{13,1},{1,5},{5,9},{9,13},{14,2},{2,6},{... | collective-permute-start | bytes 4718600 | tf_op jit(solution)/shard_map/while/body/eval_jaxpr/ppermute | solution.py:10
  51.5 35.2 %all-reduce.5.cloned.1.call-start = ((), (), s32[]{:S(2)}) async-start(), calls=%async_computation.1 | async-start | bytes 393216 | tf_op jit(solution)/shard_map/while/body/eval_jaxpr/psum | solution.py:29
  51.5 1.7 copy-start.2
  51.7 39.4 %collective-permute-start = (bf16[384,2048]{1,0:T(8,128)(2,1)S(1)}, bf16[384,2048]{1,0:T(8,128)(2,1)S(1)}, u32[]{:S(2)}, u32[]{:S(2)}) collective-permute-start(bf16[384,2048]{1,0:T(8,128)(2,1)S(1)} %copy.12), channel_id=1, source_target_pairs={{12,0},{0,4},{4,8},{8,12},{13,1},{1,5},{5,9},{9,13},{14,2},{2,6},{... | collective-permute-start | bytes 4718600 | tf_op jit(solution)/shard_map/while/body/eval_jaxpr/ppermute | solution.py:10
  91.1 35.2 %all-reduce.5.cloned.1.call-start = ((), (), s32[]{:S(2)}) async-start(), calls=%async_computation.1 | async-start | bytes 393216 | tf_op jit(solution)/shard_map/while/body/eval_jaxpr/psum | solution.py:29
  91.1 1.7 copy-start.2
  91.3 39.4 %collective-permute-start = (bf16[384,2048]{1,0:T(8,128)(2,1)S(1)}, bf16[384,2048]{1,0:T(8,128)(2,1)S(1)}, u32[]{:S(2)}, u32[]{:S(2)}) collective-permute-start(bf16[384,2048]{1,0:T(8,128)(2,1)S(1)} %copy.12), channel_id=1, source_target_pairs={{12,0},{0,4},{4,8},{8,12},{13,1},{1,5},{5,9},{9,13},{14,2},{2,6},{... | collective-permute-start | bytes 4718600 | tf_op jit(solution)/shard_map/while/body/eval_jaxpr/ppermute | solution.py:10
  130.6 34.6 %all-reduce.3.cloned.1.call-start = ((), (), s32[]{:S(2)}) async-start(), calls=%async_computation | async-start | bytes 393216 | tf_op jit(solution)/shard_map/psum | solution.py:29
  130.6 36.4 %copy-start.1 = (f32[128,2048]{1,0:T(8,128)S(1)}, f32[128,2048]{1,0:T(8,128)}, u32[]{:S(2)}) copy-start(f32[128,2048]{1,0:T(8,128)} %get-tuple-element.161) | copy-start | bytes 3145732
  130.6 36.4 %copy-start.3 = (bf16[128,2048]{1,0:T(8,128)(2,1)S(1)}, bf16[128,2048]{1,0:T(8,128)(2,1)}, u32[]{:S(2)}) copy-start(bf16[128,2048]{1,0:T(8,128)(2,1)} %get-tuple-element.272) | copy-start | bytes 1572868
Sparse Core Ops, SparseCore 0:
  14.4 33.0 all-reduce.4
  54.7 31.9 all-reduce.4
  94.2 31.9 all-reduce.4
Sparse Core Ops, SparseCore 1:
  133.4 31.8 all-reduce.2
where the time goes:
time: 177 us
  waiting for transfers between devices  130 us (73%)
  matrix products  16.5 us (9%)
  between operations  15.2 us (9%)
  local copies, waits for them, and re-layouts  8.78 us (5%)
  starting transfers between devices  6.19 us (3%)
    psum x4, waiting for transfers between devices, visit(): summed = lax.psum(part, 'pw')  130 us
    dot_general x4, matrix products, visit(): jnp.dot(summed.astype(jnp.bfloat16), piece, preferred_element_type=jnp.fl...  10.2 us
    dot_general x4, matrix products, visit(): lax.dot_general(rows, piece, (((1,), (1,)), ((), ())), preferred_element_...  6.32 us
    ppermute x3, starting transfers between devices, from_behind(): return lax.ppermute(block, axis, route)  6.18 us
    dynamic_update_slice x4, local copies, waits for them, and re-layouts, visit(): lax.dynamic_update_slice(correlation, summed, (zero_index, start))  5.54 us
  transfers between devices with their start and end apart: 7, of which 4 were waited for; matrix products, arithmetic and copies ran while one was open for 9% of the time, Pallas kernels for 0%

commit v1 on v0

--- a/solution.py
+++ b/solution.py
@@ -26,7 +26,9 @@
         part = lax.dot_general(
             rows, piece, (((1,), (1,)), ((), ())), preferred_element_type=jnp.float32
         )
-        summed = lax.psum(part, "pw")
+        summed = part
+        for hop in (1, 2):
+            summed = summed + lax.ppermute(summed, "pw", [(dev, dev ^ hop) for dev in range(4)])
         correlation = lax.dynamic_update_slice(correlation, summed, (zero_index, start))
         correction = correction + jnp.dot(
             summed.astype(jnp.bfloat16), piece, preferred_element_type=jnp.float32

time: 177 us -> 132 us (0.75)
  waiting for transfers between devices: 130 us -> 101 us
  between operations: 15.2 us -> 0.69 us
  matrix products: 16.5 us -> 11.6 us
  starting transfers between devices: 6.19 us -> 9.08 us
  other arithmetic: 0.01 us -> 2.89 us
    psum x4 -> x0, waiting for transfers between devices: 130 us -> none  [visit(): summed = lax.psum(part, 'pw')]
    ppermute x3, waiting for transfers between devices: 0.01 us -> 72.4 us  [from_behind(): return lax.ppermute(block, axis, route)]
    ppermute x0 -> x8, waiting for transfers between devices: none -> 28.2 us  [visit(): lax.ppermute(summed, 'pw', [(dev, dev ^ hop) for dev in range(4)])]
    ppermute x0 -> x8, starting transfers between devices: none -> 5.86 us  [visit(): lax.ppermute(summed, 'pw', [(dev, dev ^ hop) for dev in range(4)])]
    dynamic_update_slice x4 -> x1, local copies, waits for them, and re-layouts: 5.54 us -> 1.62 us  [visit(): lax.dynamic_update_slice(correlation, summed, (zero_index, start))]
    ppermute x3, starting transfers between devices: 6.18 us -> 3.22 us  [from_behind(): return lax.ppermute(block, axis, route)]
    dot_general x4, matrix products: 6.32 us -> 3.41 us  [visit(): lax.dot_general(rows, piece, (((1,), (1,)), ((), ())), preferred_element_...]
    dynamic_update_slice x0 -> x3, other arithmetic: none -> 2.09 us  [visit(): lax.dynamic_update_slice(correlation, summed, (zero_index, start))]
  transfers between devices with their start and end apart: 7 -> 11, of which waited for: 4 -> 11; matrix products, arithmetic and copies ran while one was open for 9% -> 8% of each run, Pallas kernels for 0% -> 0%
where the time goes in v1:
time: 132 us
  waiting for transfers between devices  101 us (77%)
  matrix products  11.6 us (9%)
  starting transfers between devices  9.08 us (7%)
  local copies, waits for them, and re-layouts  7.12 us (5%)
  other arithmetic  2.89 us (2%)
    ppermute x3, waiting for transfers between devices, from_behind(): return lax.ppermute(block, axis, route)  72.4 us
    ppermute x8, waiting for transfers between devices, visit(): lax.ppermute(summed, 'pw', [(dev, dev ^ hop) for dev in range(4)])  28.2 us
    dot_general x4, matrix products, visit(): jnp.dot(summed.astype(jnp.bfloat16), piece, preferred_element_type=jnp.fl...  8.14 us
    ppermute x8, starting transfers between devices, visit(): lax.ppermute(summed, 'pw', [(dev, dev ^ hop) for dev in range(4)])  5.86 us
    dot_general x4, matrix products, visit(): lax.dot_general(rows, piece, (((1,), (1,)), ((), ())), preferred_element_...  3.41 us
    ppermute x3, starting transfers between devices, from_behind(): return lax.ppermute(block, axis, route)  3.22 us
  transfers between devices with their start and end apart: 11, of which 11 were waited for; matrix products, arithmetic and copies ran while one was open for 8% of the time, Pallas kernels for 0%

profile of v1, /device:TPU:0, one launch (start us, length us, event | category | flops | bytes accessed | tf_op | source)
XLA Modules:
  0.0 132.0 jit_solution(16636443213059432224)
XLA Ops:
  0.7 1.0 broadcast_in_dim.6
  1.6 0.7 copy-done
  2.3 114.0 %while.20 = (s32[]{:T(128)}, bf16[384,2048]{1,0:T(8,128)(2,1)S(1)}, f32[128,1536]{1,0:T(8,128)}, f32[128,2048]{1,0:T(8,128)}, bf16[128,2048]{1,0:T(8,128)(2,1)},...) while((s32[]{:T(128)}, bf16[384,2048]{1,0:T(8,128)(2,1)S(1)}, ...), condition=%wide.region_1.2_spmd.clone, body=%wide.region_0.1_spmd.clone.sunk | while | flops 403374080 | bytes 20644284 | solution.py:44
  2.5 3.1 %collective-permute-start = (bf16[384,2048]{1,0:T(8,128)(2,1)S(1)}, bf16[384,2048]{1,0:T(8,128)(2,1)S(1)}, u32[]{:S(2)}, u32[]{:S(2)}) collective-permute-start(bf16[384,2048]{1,0:T(8,128)(2,1)S(1)} %copy.11), channel_id=1, source_target_pairs={{12,0},{0,4},{4,8},{8,12},{13,1},{1,5},{5,9},{9,13},{14,2},{2,6},{... | collective-permute-start | bytes 4718600 | tf_op jit(solution)/shard_map/while/body/eval_jaxpr/ppermute | solution.py:10
  6.3 1.4 %collective-permute-done.1 = f32[128,384]{1,0:T(8,128)S(1)} collective-permute-done((f32[128,384]{1,0:T(8,128)S(1)}, f32[128,384]{1,0:T(8,128)S(1)}, u32[]{:S(2)}, u32[]{:S(2)}) %collective-permute-start.1) | collective-permute-done | bytes 196640 | tf_op jit(solution)/shard_map/while/body/eval_jaxpr/ppermute | solution.py:31
  7.7 1.6 %collective-permute-start.2 = (f32[128,384]{1,0:T(8,128)S(1)}, f32[128,384]{1,0:T(8,128)S(1)}, u32[]{:S(2)}, u32[]{:S(2)}) collective-permute-start(f32[128,384]{1,0:T(8,128)S(1)} %add.127), channel_id=1, source_target_pairs={{0,2},{1,3},{2,0},{3,1},{4,6},{5,7},{6,4},{7,5},{8,10},{9,11},{10,... | collective-permute-start | bytes 589832 | tf_op jit(solution)/shard_map/while/body/eval_jaxpr/ppermute | solution.py:31
  9.3 5.5 %collective-permute-done.2 = f32[128,384]{1,0:T(8,128)S(1)} collective-permute-done((f32[128,384]{1,0:T(8,128)S(1)}, f32[128,384]{1,0:T(8,128)S(1)}, u32[]{:S(2)}, u32[]{:S(2)}) %collective-permute-start.2) | collective-permute-done | bytes 196640 | tf_op jit(solution)/shard_map/while/body/eval_jaxpr/ppermute | solution.py:31
  14.8 0.7 add_dynamic-update-slice_fusion.2
  15.5 1.4 %convolution_add_fusion.3 = f32[128,2048]{1,0:T(8,128)} fusion(bf16[384,2048]{1,0:T(8,128)(2,1)S(1)} %copy.11, f32[128,2048]{1,0:T(8,128)} %get-tuple-element.247, pred[]{:T(512)S(6)} %compare.5, f32[128,384]{1,0:T(8,128)S(1)} %add.127, f32[128,384]{1,0:T(8,128)S(1)} %collective-permute-done.2), kind=kOutput, calls=%fused_computation.clone.1 | convolution fusion | flops 201949184 | bytes 4063233 | tf_op jit(solution)/shard_map/while/body/eval_jaxpr/dot_general | solution.py:33
  16.9 25.1 %collective-permute-done = bf16[384,2048]{1,0:T(8,128)(2,1)S(1)} collective-permute-done((bf16[384,2048]{1,0:T(8,128)(2,1)S(1)}, bf16[384,2048]{1,0:T(8,128)(2,1)S(1)}, u32[]{:S(2)}, u32[]{:S(2)}) %collective-permute-start) | collective-permute-done | bytes 1572896 | tf_op jit(solution)/shard_map/while/body/eval_jaxpr/ppermute | solution.py:10
  42.3 0.8 copy-done.2
  43.8 1.4 %collective-permute-done.1 = f32[128,384]{1,0:T(8,128)S(1)} collective-permute-done((f32[128,384]{1,0:T(8,128)S(1)}, f32[128,384]{1,0:T(8,128)S(1)}, u32[]{:S(2)}, u32[]{:S(2)}) %collective-permute-start.1) | collective-permute-done | bytes 196640 | tf_op jit(solution)/shard_map/while/body/eval_jaxpr/ppermute | solution.py:31
  45.2 1.6 %collective-permute-start.2 = (f32[128,384]{1,0:T(8,128)S(1)}, f32[128,384]{1,0:T(8,128)S(1)}, u32[]{:S(2)}, u32[]{:S(2)}) collective-permute-start(f32[128,384]{1,0:T(8,128)S(1)} %add.127), channel_id=1, source_target_pairs={{0,2},{1,3},{2,0},{3,1},{4,6},{5,7},{6,4},{7,5},{8,10},{9,11},{10,... | collective-permute-start | bytes 589832 | tf_op jit(solution)/shard_map/while/body/eval_jaxpr/ppermute | solution.py:31
  46.8 5.5 %collective-permute-done.2 = f32[128,384]{1,0:T(8,128)S(1)} collective-permute-done((f32[128,384]{1,0:T(8,128)S(1)}, f32[128,384]{1,0:T(8,128)S(1)}, u32[]{:S(2)}, u32[]{:S(2)}) %collective-permute-start.2) | collective-permute-done | bytes 196640 | tf_op jit(solution)/shard_map/while/body/eval_jaxpr/ppermute | solution.py:31
  52.2 0.7 add_dynamic-update-slice_fusion.2
  52.9 2.6 %convolution_add_fusion.3 = f32[128,2048]{1,0:T(8,128)} fusion(bf16[384,2048]{1,0:T(8,128)(2,1)S(1)} %copy.11, f32[128,2048]{1,0:T(8,128)} %get-tuple-element.247, pred[]{:T(512)S(6)} %compare.5, f32[128,384]{1,0:T(8,128)S(1)} %add.127, f32[128,384]{1,0:T(8,128)S(1)} %collective-permute-done.2), kind=kOutput, calls=%fused_computation.clone.1 | convolution fusion | flops 201949184 | bytes 4063233 | tf_op jit(solution)/shard_map/while/body/eval_jaxpr/dot_general | solution.py:33
  55.6 24.1 %collective-permute-done = bf16[384,2048]{1,0:T(8,128)(2,1)S(1)} collective-permute-done((bf16[384,2048]{1,0:T(8,128)(2,1)S(1)}, bf16[384,2048]{1,0:T(8,128)(2,1)S(1)}, u32[]{:S(2)}, u32[]{:S(2)}) %collective-permute-start) | collective-permute-done | bytes 1572896 | tf_op jit(solution)/shard_map/while/body/eval_jaxpr/ppermute | solution.py:10
  79.8 0.8 copy-done.2
  81.3 1.4 %collective-permute-done.1 = f32[128,384]{1,0:T(8,128)S(1)} collective-permute-done((f32[128,384]{1,0:T(8,128)S(1)}, f32[128,384]{1,0:T(8,128)S(1)}, u32[]{:S(2)}, u32[]{:S(2)}) %collective-permute-start.1) | collective-permute-done | bytes 196640 | tf_op jit(solution)/shard_map/while/body/eval_jaxpr/ppermute | solution.py:31
  82.8 1.3 %collective-permute-start.2 = (f32[128,384]{1,0:T(8,128)S(1)}, f32[128,384]{1,0:T(8,128)S(1)}, u32[]{:S(2)}, u32[]{:S(2)}) collective-permute-start(f32[128,384]{1,0:T(8,128)S(1)} %add.127), channel_id=1, source_target_pairs={{0,2},{1,3},{2,0},{3,1},{4,6},{5,7},{6,4},{7,5},{8,10},{9,11},{10,... | collective-permute-start | bytes 589832 | tf_op jit(solution)/shard_map/while/body/eval_jaxpr/ppermute | solution.py:31
  84.1 5.7 %collective-permute-done.2 = f32[128,384]{1,0:T(8,128)S(1)} collective-permute-done((f32[128,384]{1,0:T(8,128)S(1)}, f32[128,384]{1,0:T(8,128)S(1)}, u32[]{:S(2)}, u32[]{:S(2)}) %collective-permute-start.2) | collective-permute-done | bytes 196640 | tf_op jit(solution)/shard_map/while/body/eval_jaxpr/ppermute | solution.py:31
  89.8 0.7 add_dynamic-update-slice_fusion.2
  90.5 2.6 %convolution_add_fusion.3 = f32[128,2048]{1,0:T(8,128)} fusion(bf16[384,2048]{1,0:T(8,128)(2,1)S(1)} %copy.11, f32[128,2048]{1,0:T(8,128)} %get-tuple-element.247, pred[]{:T(512)S(6)} %compare.5, f32[128,384]{1,0:T(8,128)S(1)} %add.127, f32[128,384]{1,0:T(8,128)S(1)} %collective-permute-done.2), kind=kOutput, calls=%fused_computation.clone.1 | convolution fusion | flops 201949184 | bytes 4063233 | tf_op jit(solution)/shard_map/while/body/eval_jaxpr/dot_general | solution.py:33
  93.1 23.2 %collective-permute-done = bf16[384,2048]{1,0:T(8,128)(2,1)S(1)} collective-permute-done((bf16[384,2048]{1,0:T(8,128)(2,1)S(1)}, bf16[384,2048]{1,0:T(8,128)(2,1)S(1)}, u32[]{:S(2)}, u32[]{:S(2)}) %collective-permute-start) | collective-permute-done | bytes 1572896 | tf_op jit(solution)/shard_map/while/body/eval_jaxpr/ppermute | solution.py:10
  116.3 1.6 %convolution_bitcast_fusion = f32[128,384]{0,1:T(8,128)S(1)} fusion(bf16[384,2048]{1,0:T(8,128)(2,1)S(1)} %get-tuple-element.160, bf16[1,128,2048]{2,1,0:T(8,128)(2,1)} %bitcast.23), kind=kOutput, calls=%fused_computation.7 | convolution fusion | flops 201326592 | bytes 2293760 | tf_op jit(solution)/shard_map/dot_general | solution.py:26
  118.1 1.4 %collective-permute-done.3 = f32[128,384]{0,1:T(8,128)S(1)} collective-permute-done((f32[128,384]{0,1:T(8,128)S(1)}, f32[128,384]{0,1:T(8,128)S(1)}, u32[]{:S(2)}, u32[]{:S(2)}) %collective-permute-start.3) | collective-permute-done | bytes 196640 | tf_op jit(solution)/shard_map/ppermute | solution.py:31
  119.5 1.1 collective-permute-start.4
  120.6 5.9 %collective-permute-done.4 = f32[128,384]{0,1:T(8,128)S(1)} collective-permute-done((f32[128,384]{0,1:T(8,128)S(1)}, f32[128,384]{0,1:T(8,128)S(1)}, u32[]{:S(2)}, u32[]{:S(2)}) %collective-permute-start.4) | collective-permute-done | bytes 196640 | tf_op jit(solution)/shard_map/ppermute | solution.py:31
  126.5 0.7 add_bitcast_fusion
  127.2 1.7 %copy.4 = f32[1,128,384]{2,1,0:T(8,128)} copy(f32[1,128,384]{1,2,0:T(8,128)} %add_bitcast_fusion) | data formatting | bytes 393216 | tf_op jit(solution)/shard_map/reshape | solution.py:49
  128.9 1.6 %constant_dynamic-update-slice_fusion = f32[1,128,1536]{2,1,0:T(8,128)} fusion(f32[1,128,1536]{2,1,0:T(8,128)} %bitcast.25, f32[1,128,384]{2,1,0:T(8,128)} %copy.4, s32[]{:T(128)S(6)} %select_n.38), kind=kLoop, calls=%fused_computation.11 | loop fusion | bytes 393220 | tf_op jit(solution)/shard_map/dynamic_update_slice | solution.py:32
  130.6 1.4 %fusion.3 = f32[1,128,2048]{2,1,0:T(8,128)} fusion(f32[128,2048]{1,0:T(8,128)S(1)} %copy-done.1, bf16[384,2048]{1,0:T(8,128)(2,1)S(1)} %get-tuple-element.160, f32[128,384]{0,1:T(8,128)S(1)} %add.87, f32[128,384]{0,1:T(8,128)S(1)} %collective-permute-done.4, bf16[1,128,2048]{2,1,0:T(8,128)(2,1)S(1)} %bitcast.24), kind=kOutput, calls=%fused_computation.6 | convolution fusion | flops 202211328 | bytes 4587520 | tf_op jit(solution)/shard_map/dot_general | solution.py:33
  (26 shorter events, 2.8 us)
Async XLA Ops:
  0.6 1.7 %copy-start = (bf16[384,2048]{1,0:T(8,128)(2,1)S(1)}, bf16[384,2048]{1,0:T(8,128)(2,1)}, u32[]{:S(2)}) copy-start(bf16[384,2048]{1,0:T(8,128)(2,1)} %param.4) | copy-start | bytes 4718596
  2.3 3.3 %copy-start.2 = (bf16[128,2048]{1,0:T(8,128)(2,1)S(1)}, bf16[128,2048]{1,0:T(8,128)(2,1)}, u32[]{:S(2)}) copy-start(bf16[128,2048]{1,0:T(8,128)(2,1)} %get-tuple-element.260) | copy-start | bytes 1572868 | tf_op jit(solution)/shard_map/while
  2.5 39.5 %collective-permute-start = (bf16[384,2048]{1,0:T(8,128)(2,1)S(1)}, bf16[384,2048]{1,0:T(8,128)(2,1)S(1)}, u32[]{:S(2)}, u32[]{:S(2)}) collective-permute-start(bf16[384,2048]{1,0:T(8,128)(2,1)S(1)} %copy.11), channel_id=1, source_target_pairs={{12,0},{0,4},{4,8},{8,12},{13,1},{1,5},{5,9},{9,13},{14,2},{2,6},{... | collective-permute-start | bytes 4718600 | tf_op jit(solution)/shard_map/while/body/eval_jaxpr/ppermute | solution.py:10
  6.2 1.5 %collective-permute-start.1 = (f32[128,384]{1,0:T(8,128)S(1)}, f32[128,384]{1,0:T(8,128)S(1)}, u32[]{:S(2)}, u32[]{:S(2)}) collective-permute-start(f32[128,384]{1,0:T(8,128)S(1)} %fusion.22), channel_id=1, source_target_pairs={{0,1},{1,0},{2,3},{3,2},{4,5},{5,4},{6,7},{7,6},{8,9},{9,8},{10,11... | collective-permute-start | bytes 589832 | tf_op jit(solution)/shard_map/while/body/eval_jaxpr/ppermute | solution.py:31
  7.7 7.0 %collective-permute-start.2 = (f32[128,384]{1,0:T(8,128)S(1)}, f32[128,384]{1,0:T(8,128)S(1)}, u32[]{:S(2)}, u32[]{:S(2)}) collective-permute-start(f32[128,384]{1,0:T(8,128)S(1)} %add.127), channel_id=1, source_target_pairs={{0,2},{1,3},{2,0},{3,1},{4,6},{5,7},{6,4},{7,5},{8,10},{9,11},{10,... | collective-permute-start | bytes 589832 | tf_op jit(solution)/shard_map/while/body/eval_jaxpr/ppermute | solution.py:31
  42.0 1.0 copy-start.2
  42.2 37.4 %collective-permute-start = (bf16[384,2048]{1,0:T(8,128)(2,1)S(1)}, bf16[384,2048]{1,0:T(8,128)(2,1)S(1)}, u32[]{:S(2)}, u32[]{:S(2)}) collective-permute-start(bf16[384,2048]{1,0:T(8,128)(2,1)S(1)} %copy.11), channel_id=1, source_target_pairs={{12,0},{0,4},{4,8},{8,12},{13,1},{1,5},{5,9},{9,13},{14,2},{2,6},{... | collective-permute-start | bytes 4718600 | tf_op jit(solution)/shard_map/while/body/eval_jaxpr/ppermute | solution.py:10
  43.7 1.5 %collective-permute-start.1 = (f32[128,384]{1,0:T(8,128)S(1)}, f32[128,384]{1,0:T(8,128)S(1)}, u32[]{:S(2)}, u32[]{:S(2)}) collective-permute-start(f32[128,384]{1,0:T(8,128)S(1)} %fusion.22), channel_id=1, source_target_pairs={{0,1},{1,0},{2,3},{3,2},{4,5},{5,4},{6,7},{7,6},{8,9},{9,8},{10,11... | collective-permute-start | bytes 589832 | tf_op jit(solution)/shard_map/while/body/eval_jaxpr/ppermute | solution.py:31
  45.2 7.0 %collective-permute-start.2 = (f32[128,384]{1,0:T(8,128)S(1)}, f32[128,384]{1,0:T(8,128)S(1)}, u32[]{:S(2)}, u32[]{:S(2)}) collective-permute-start(f32[128,384]{1,0:T(8,128)S(1)} %add.127), channel_id=1, source_target_pairs={{0,2},{1,3},{2,0},{3,1},{4,6},{5,7},{6,4},{7,5},{8,10},{9,11},{10,... | collective-permute-start | bytes 589832 | tf_op jit(solution)/shard_map/while/body/eval_jaxpr/ppermute | solution.py:31
  79.6 1.0 copy-start.2
  79.8 36.6 %collective-permute-start = (bf16[384,2048]{1,0:T(8,128)(2,1)S(1)}, bf16[384,2048]{1,0:T(8,128)(2,1)S(1)}, u32[]{:S(2)}, u32[]{:S(2)}) collective-permute-start(bf16[384,2048]{1,0:T(8,128)(2,1)S(1)} %copy.11), channel_id=1, source_target_pairs={{12,0},{0,4},{4,8},{8,12},{13,1},{1,5},{5,9},{9,13},{14,2},{2,6},{... | collective-permute-start | bytes 4718600 | tf_op jit(solution)/shard_map/while/body/eval_jaxpr/ppermute | solution.py:10
  81.3 1.5 %collective-permute-start.1 = (f32[128,384]{1,0:T(8,128)S(1)}, f32[128,384]{1,0:T(8,128)S(1)}, u32[]{:S(2)}, u32[]{:S(2)}) collective-permute-start(f32[128,384]{1,0:T(8,128)S(1)} %fusion.22), channel_id=1, source_target_pairs={{0,1},{1,0},{2,3},{3,2},{4,5},{5,4},{6,7},{7,6},{8,9},{9,8},{10,11... | collective-permute-start | bytes 589832 | tf_op jit(solution)/shard_map/while/body/eval_jaxpr/ppermute | solution.py:31
  82.8 7.0 %collective-permute-start.2 = (f32[128,384]{1,0:T(8,128)S(1)}, f32[128,384]{1,0:T(8,128)S(1)}, u32[]{:S(2)}, u32[]{:S(2)}) collective-permute-start(f32[128,384]{1,0:T(8,128)S(1)} %add.127), channel_id=1, source_target_pairs={{0,2},{1,3},{2,0},{3,1},{4,6},{5,7},{6,4},{7,5},{8,10},{9,11},{10,... | collective-permute-start | bytes 589832 | tf_op jit(solution)/shard_map/while/body/eval_jaxpr/ppermute | solution.py:31
  117.9 12.6 %copy-start.1 = (f32[128,2048]{1,0:T(8,128)S(1)}, f32[128,2048]{1,0:T(8,128)}, u32[]{:S(2)}) copy-start(f32[128,2048]{1,0:T(8,128)} %get-tuple-element.161) | copy-start | bytes 3145732
  118.0 12.6 %copy-start.3 = (bf16[128,2048]{1,0:T(8,128)(2,1)S(1)}, bf16[128,2048]{1,0:T(8,128)(2,1)}, u32[]{:S(2)}) copy-start(bf16[128,2048]{1,0:T(8,128)(2,1)} %get-tuple-element.271) | copy-start | bytes 1572868
  118.0 1.5 %collective-permute-start.3 = (f32[128,384]{0,1:T(8,128)S(1)}, f32[128,384]{0,1:T(8,128)S(1)}, u32[]{:S(2)}, u32[]{:S(2)}) collective-permute-start(f32[128,384]{0,1:T(8,128)S(1)} %convolution_bitcast_fusion), channel_id=1, source_target_pairs={{0,1},{1,0},{2,3},{3,2},{4,5},{5,4},{6,7},{7,6},{8,9},{9,8},{10,11... | collective-permute-start | bytes 589832 | tf_op jit(solution)/shard_map/ppermute | solution.py:31
  119.5 7.0 %collective-permute-start.4 = (f32[128,384]{0,1:T(8,128)S(1)}, f32[128,384]{0,1:T(8,128)S(1)}, u32[]{:S(2)}, u32[]{:S(2)}) collective-permute-start(f32[128,384]{0,1:T(8,128)S(1)} %add.87), channel_id=1, source_target_pairs={{0,2},{1,3},{2,0},{3,1},{4,6},{5,7},{6,4},{7,5},{8,10},{9,11},{10,... | collective-permute-start | bytes 589832 | tf_op jit(solution)/shard_map/ppermute | solution.py:31
